TPU v7x, 32 devices: a whole 2x2x4 slice. The times are simulated.
32 devices in a mesh: dom: 8 (over z, y), feat: 4 (over x, core).
Axes of the slice: x: 2, y: 2, z: 4, core: 2. Of those that a mesh axis runs over, the one named last changes fastest.
Arguments:
- feats: bfloat16 [16384, 1024], P('dom', 'feat'), may hold values from -6 to 6
- projection: bfloat16 [1024, 512], P('feat'), may hold values from -0.1875 to 0.1875
- tiles: bfloat16 [1024, 4, 128, 128], P(('dom', 'feat')), may hold values from -0.25 to 0.25
- slot_owner: int32 [1024, 1], P(('dom', 'feat')), may hold values from 0 to 7; in each aligned block of 32 rows (0 to 31, 32 to 63, ...) at most 8 rows name the same one
- slot_block: int32 [1024, 1], P(('dom', 'feat')), may hold values from 0 to 3
- source_block: int32 [1024, 4], P(('dom', 'feat')), may hold values from 0 to 3
- counts: int32 [16384], P(('dom', 'feat')), may hold values from 1 to 4
- out_grad: bfloat16 [16384, 256], P(('dom', 'feat')), may hold values from -0.046875 to 0.046875
Outputs:
- activated: bfloat16 [16384, 256], P(('dom', 'feat'))
- weight_grad: float32 [1024, 512], P('feat')
Inputs may be any that keep to these rules, and one draw needn't show every extreme that they name: `slot_owner`: among the 32 sent rows of one device, no dom index is named more than 8 times; some device names one exactly 8 times.
All inputs are finite; a program needn't handle non-finite values.
Results may differ from a plain program's by a relative error of at most 0.0059.
Values may be sent and summed in bfloat16 or wider, within the bound.
No kernel may reach another device: no remote copies, remote signals or barrier semaphores. Data moves between devices by JAX's collectives and lax.ppermute only.
A program may use at most 128 MiB of HBM per device.

v0:
```python
import jax
import jax.numpy as jnp
from jax import lax
from jax.sharding import PartitionSpec as P


def local(feats, projection, tiles, slot_owner, slot_block, source_block, counts, out_grad):
    tile_size = tiles.shape[-1]
    slot_count = tiles.shape[0]
    per_slot = tiles.shape[1]
    out_width = out_grad.shape[1]
    node_rows = out_grad.shape[0]
    block_count = node_rows // tile_size
    dom_count = lax.axis_size("dom")
    capacity = max(2, 2 * slot_count // dom_count)
    flat_width = tile_size * out_width
    own_rows = lax.all_to_all(feats, "feat", split_axis=0, concat_axis=1, tiled=True)
    full_weight = lax.all_gather(projection, "feat", axis=0, tiled=True)
    projected = jnp.dot(own_rows, full_weight, preferred_element_type=jnp.float32).astype(
        jnp.bfloat16
    )
    neighbour = projected[:, :out_width].reshape(block_count, tile_size, out_width)
    self_part = projected[:, out_width:]
    picked = neighbour[source_block]
    contribution = jnp.einsum("skij,skjh->sih", tiles, picked, preferred_element_type=jnp.float32)
    contribution = contribution.astype(jnp.bfloat16).reshape(slot_count, flat_width)
    slot_dest = slot_owner[:, 0]
    dest_block = slot_block[:, 0]
    dest_hot = (slot_dest[:, None] == jnp.arange(dom_count, dtype=jnp.int32)[None, :]).astype(
        jnp.int32
    )
    before = jnp.cumsum(dest_hot, axis=0) - dest_hot
    position = jnp.sum(before * dest_hot, axis=1)
    slot_index = slot_dest * capacity + position
    placing = jnp.arange(dom_count * capacity, dtype=jnp.int32)[:, None] == slot_index[None, :]
    outgoing = jnp.dot(
        placing.astype(jnp.bfloat16), contribution, preferred_element_type=jnp.float32
    )
    outgoing = outgoing.astype(jnp.bfloat16).reshape(dom_count, capacity, flat_width)
    labels = jnp.sum(placing.astype(jnp.int32) * (dest_block + 1)[None, :], axis=1) - 1
    labels = labels.reshape(dom_count, capacity)
    incoming, got_labels = (
        lax.all_to_all(outgoing, "dom", split_axis=0, concat_axis=0, tiled=True),
        lax.all_to_all(labels, "dom", split_axis=0, concat_axis=0, tiled=True),
    )
    incoming = incoming.reshape(dom_count * capacity, flat_width)
    receive_hot = (
        jnp.arange(block_count, dtype=jnp.int32)[:, None] == got_labels.reshape(-1)[None, :]
    ).astype(jnp.bfloat16)
    summed = jnp.dot(receive_hot, incoming, preferred_element_type=jnp.float32).reshape(
        node_rows, out_width
    )
    degree = counts.astype(jnp.float32)[:, None]
    preact = summed / degree + self_part.astype(jnp.float32)
    sigma = jax.nn.sigmoid(preact)
    activated = (preact * sigma).astype(jnp.bfloat16)
    grad_pre = out_grad.astype(jnp.float32) * sigma * (1.0 + preact * (1.0 - sigma))
    grad_self = grad_pre.astype(jnp.bfloat16)
    grad_sum = (grad_pre / degree).astype(jnp.bfloat16).reshape(block_count, flat_width)
    sending_back = jnp.dot(receive_hot.T, grad_sum, preferred_element_type=jnp.float32)
    sending_back = sending_back.astype(jnp.bfloat16).reshape(dom_count, capacity, flat_width)
    returned = lax.all_to_all(sending_back, "dom", split_axis=0, concat_axis=0, tiled=True).reshape(
        dom_count * capacity, flat_width
    )
    slot_grad = jnp.dot(
        placing.T.astype(jnp.bfloat16), returned, preferred_element_type=jnp.float32
    )
    slot_grad = slot_grad.astype(jnp.bfloat16).reshape(slot_count, tile_size, out_width)
    products = jnp.einsum("skij,sih->skjh", tiles, slot_grad, preferred_element_type=jnp.float32)
    source_hot = (
        jnp.arange(block_count, dtype=jnp.int32)[:, None] == source_block.reshape(-1)[None, :]
    ).astype(jnp.float32)
    flat_products = products.reshape(slot_count * per_slot, tile_size, out_width)
    grad_neigh = jnp.einsum(
        "bn,njh->bjh", source_hot, flat_products, precision=lax.Precision.HIGHEST
    )
    grad_neigh = grad_neigh.astype(jnp.bfloat16).reshape(node_rows, out_width)
    grad_proj = jnp.concatenate([grad_neigh, grad_self], axis=1)
    partial_grad = lax.psum_scatter(
        lax.dot_general(
            own_rows, grad_proj, (((0,), (0,)), ((), ())), preferred_element_type=jnp.float32
        ),
        "feat",
        scatter_dimension=0,
        tiled=True,
    )
    weight_grad = lax.psum(partial_grad, "dom")
    return (activated, weight_grad)


def solution(mesh):
    placed = (
        P("dom", "feat"),
        P("feat", None),
        P(("dom", "feat"), None, None, None),
        P(("dom", "feat"), None),
        P(("dom", "feat"), None),
        P(("dom", "feat"), None),
        P(("dom", "feat")),
        P(("dom", "feat"), None),
    )
    return jax.shard_map(
        local,
        mesh=mesh,
        in_specs=placed,
        out_specs=(P(("dom", "feat"), None), P("feat", None)),
        check_vma=False,
    )
```

profile of v0, /device:TPU:0, one launch (start us, length us, event | category | flops | bytes accessed | tf_op | source)
XLA Modules:
  0.0 421.0 jit_solution(1731139456741465177)
XLA Ops:
  7.9 4.2 %all-to-all-start.1 = ((bf16[4,512,256]{2,1,0:T(8,128)(2,1)}), bf16[4,512,256]{2,1,0:T(8,128)(2,1)S(1)}, u32[]{:S(2)}, u32[]{:S(2)}) async-start(bf16[4,512,256]{2,1,0:T(8,128)(2,1)} %bitcast.67), calls=%async_computation.1 | async-start | bytes 2097152 | tf_op jit(solution)/shard_map/all_to_all | solution.py:17
  14.5 0.8 select_reduce_fusion.1
  16.8 15.2 %all-to-all-done.1 = bf16[4,512,256]{2,1,0:T(8,128)(2,1)S(1)} async-done(((bf16[4,512,256]{2,1,0:T(8,128)(2,1)}), bf16[4,512,256]{2,1,0:T(8,128)(2,1)S(1)}, u32[]{:S(2)}, u32[]{:S(2)}) %all-to-all-start.1) | async-done | bytes 1048608 | tf_op jit(solution)/shard_map/all_to_all | solution.py:17
  32.0 6.8 %all-to-all-start = ((s32[8,1,8]{2,1,0:T(1,128)}), s32[8,1,8]{2,1,0:T(1,128)S(1)}, u32[]{:S(2)}, u32[]{:S(2)}) async-start(s32[8,1,8]{2,1,0:T(1,128)} %bitcast.2), calls=%async_computation | async-start | bytes 8192 | tf_op jit(solution)/shard_map/all_to_all | solution.py:44
  39.3 2.0 convolution_convert_fusion.3
  41.3 6.5 %gather_fusion = bf16[128,128,256]{2,1,0:T(8,128)(2,1)} fusion(bf16[4,128,256]{2,1,0:T(8,128)(2,1)S(1)} %bitcast.56, s32[1024]{0:T(1024)S(1)} %pad_clamp_fusion), kind=kCustom, calls=%fused_computation | custom fusion | bytes 16777728 | tf_op jit(solution)/shard_map/gather | solution.py:24
  47.8 7.0 %fusion.7 = bf16[32,128,256]{1,2,0:T(8,128)(2,1)S(1)} fusion(bf16[32,4,128,256]{3,2,1,0:T(8,128)(2,1)} %bitcast.58, bf16[32,4,128,128]{3,2,1,0:T(8,128)(2,1)} %param.10), kind=kOutput, calls=%fused_computation.13 | convolution fusion | flops 1074790400 | bytes 14680064 | tf_op jit(solution)/shard_map/skij,skjh->sih/dot_general | solution.py:25
  54.8 2.9 copy.58
  57.7 4.9 %fusion = bf16[8,8,32768]{2,1,0:T(8,128)(2,1)} fusion(bf16[32,32768]{1,0:T(8,128)(2,1)} %bitcast.61, s32[32]{0:T(128)S(1)} %multiply_add_fusion), kind=kOutput, calls=%fused_computation.3 | convolution fusion | flops 136316928 | bytes 6291584 | tf_op jit(solution)/shard_map/dot_general | solution.py:36
  62.6 6.2 %all-to-all-start.2 = ((bf16[8,8,32768]{2,1,0:T(8,128)(2,1)}), bf16[8,8,32768]{2,1,0:T(8,128)(2,1)}, u32[]{:S(2)}, u32[]{:S(2)}) async-start(bf16[8,8,32768]{2,1,0:T(8,128)(2,1)} %fusion), calls=%async_computation.2 | async-start | bytes 8388608 | tf_op jit(solution)/shard_map/all_to_all | solution.py:43
  70.1 90.7 %all-to-all-done.2 = bf16[8,8,32768]{2,1,0:T(8,128)(2,1)} async-done(((bf16[8,8,32768]{2,1,0:T(8,128)(2,1)}), bf16[8,8,32768]{2,1,0:T(8,128)(2,1)}, u32[]{:S(2)}, u32[]{:S(2)}) %all-to-all-start.2) | async-done | bytes 4194336 | tf_op jit(solution)/shard_map/all_to_all | solution.py:43
  160.8 2.8 fusion.3
  164.0 1.1 divide_convert_fusion
  165.3 3.3 fusion.1
  168.6 4.7 %all-to-all-start.3 = ((bf16[8,8,32768]{2,1,0:T(8,128)(2,1)}), bf16[8,8,32768]{2,1,0:T(8,128)(2,1)}, u32[]{:S(2)}, u32[]{:S(2)}) async-start(bf16[8,8,32768]{2,1,0:T(8,128)(2,1)} %fusion.1), calls=%async_computation.3 | async-start | bytes 8388608 | tf_op jit(solution)/shard_map/all_to_all | solution.py:62
  173.7 92.1 %all-to-all-done.3 = bf16[8,8,32768]{2,1,0:T(8,128)(2,1)} async-done(((bf16[8,8,32768]{2,1,0:T(8,128)(2,1)}), bf16[8,8,32768]{2,1,0:T(8,128)(2,1)}, u32[]{:S(2)}, u32[]{:S(2)}) %all-to-all-start.3) | async-done | bytes 4194336 | tf_op jit(solution)/shard_map/all_to_all | solution.py:62
  265.9 3.1 convolution_convert_fusion.2
  269.5 8.1 %fusion.5 = f32[32,256,4,128]{3,1,2,0:T(8,128)} fusion(bf16[32,4,128,128]{3,2,1,0:T(8,128)(2,1)S(1)} %copy-done, bf16[32,128,256]{2,1,0:T(8,128)(2,1)S(1)} %bitcast.62), kind=kOutput, calls=%fused_computation.10 | convolution fusion | flops 1073741824 | bytes 23068672 | tf_op jit(solution)/shard_map/skij,sih->skjh/dot_general | solution.py:69
  277.6 17.6 %copy.51 = f32[128,128,256]{2,0,1:T(8,128)} copy(f32[128,128,256]{1,2,0:T(8,128)} %bitcast.57) | data formatting | bytes 33554432 | tf_op jit(solution)/shard_map/reshape | solution.py:73
  295.2 9.0 %convolution_convert_fusion.4 = bf16[4,128,256]{2,0,1:T(4,128)(2,1)S(1)} fusion(f32[128,128,256]{2,0,1:T(8,128)} %copy.51, s32[128]{0:T(128)S(1)} %eq.67), kind=kOutput, calls=%fused_computation.15 | convolution fusion | flops 201458176 | bytes 17039872 | tf_op jit(solution)/shard_map/bn,njh->bjh/dot_general | solution.py:74
  304.3 2.1 convolution_bitcast_fusion
  306.5 29.7 %reduce-scatter.2.cloned.1.call-done = f32[256,512]{0,1:T(8,128)} async-done(((f32[1024,512]{0,1:T(8,128)}), f32[256,512]{0,1:T(8,128)}) %reduce-scatter.2.cloned.1.call-update) | async-done | bytes 524304 | tf_op jit(solution)/shard_map/reduce_scatter | solution.py:79
  336.2 76.2 %all-reduce.2.cloned.1.call-done = f32[256,512]{0,1:T(8,128)} async-done(((f32[256,512]{0,1:T(8,128)}), f32[256,512]{0,1:T(8,128)}) %all-reduce.2.cloned.1.call-update) | async-done | bytes 524304 | tf_op jit(solution)/shard_map/psum | solution.py:87
  412.5 2.0 copy.53
  (43 shorter events, 7.9 us)
Async XLA Ops:
  7.2 32.2 %all-gather.2.cloned.1.call-start = ((), (), s32[]{:S(2)}) async-start(), calls=%async_computation.5 | async-start | bytes 1310720 | tf_op jit(solution)/shard_map/all_gather | solution.py:18
  7.9 24.1 %all-to-all-start.1 = ((bf16[4,512,256]{2,1,0:T(8,128)(2,1)}), bf16[4,512,256]{2,1,0:T(8,128)(2,1)S(1)}, u32[]{:S(2)}, u32[]{:S(2)}) async-start(bf16[4,512,256]{2,1,0:T(8,128)(2,1)} %bitcast.67), calls=%async_computation.1 | async-start | bytes 2097152 | tf_op jit(solution)/shard_map/all_to_all | solution.py:17
  32.0 30.6 %all-to-all-start = ((s32[8,1,8]{2,1,0:T(1,128)}), s32[8,1,8]{2,1,0:T(1,128)S(1)}, u32[]{:S(2)}, u32[]{:S(2)}) async-start(s32[8,1,8]{2,1,0:T(1,128)} %bitcast.2), calls=%async_computation | async-start | bytes 8192 | tf_op jit(solution)/shard_map/all_to_all | solution.py:44
  41.3 6.5 %copy-start.1 = (bf16[512,512]{1,0:T(8,128)(2,1)}, bf16[512,512]{1,0:T(8,128)(2,1)S(1)}, u32[]{:S(2)}) copy-start(bf16[512,512]{1,0:T(8,128)(2,1)S(1)} %convolution_convert_fusion.3) | copy-start | bytes 1572868
  62.6 6.2 %copy-start.5 = (s32[512]{0:T(512)S(1)}, s32[512]{0:T(512)}, u32[]{:S(2)}) copy-start(s32[512]{0:T(512)} %param.14) | copy-start | bytes 6148
  62.6 98.2 %all-to-all-start.2 = ((bf16[8,8,32768]{2,1,0:T(8,128)(2,1)}), bf16[8,8,32768]{2,1,0:T(8,128)(2,1)}, u32[]{:S(2)}, u32[]{:S(2)}) async-start(bf16[8,8,32768]{2,1,0:T(8,128)(2,1)} %fusion), calls=%async_computation.2 | async-start | bytes 8388608 | tf_op jit(solution)/shard_map/all_to_all | solution.py:43
  68.8 95.2 %copy-start.2 = (bf16[512,512]{1,0:T(8,128)(2,1)S(1)}, bf16[512,512]{1,0:T(8,128)(2,1)}, u32[]{:S(2)}) copy-start(bf16[512,512]{1,0:T(8,128)(2,1)} %copy-done.1) | copy-start | bytes 1572868
  68.8 95.2 %copy-start.3 = (bf16[512,256]{1,0:T(8,128)(2,1)S(1)}, bf16[512,256]{1,0:T(8,128)(2,1)}, u32[]{:S(2)}) copy-start(bf16[512,256]{1,0:T(8,128)(2,1)} %param.15) | copy-start | bytes 786436
  168.6 4.9 %copy-start.4 = (s32[32,4]{0,1:T(4,128)S(1)}, s32[32,4]{0,1:T(4,128)}, u32[]{:S(2)}) copy-start(s32[32,4]{0,1:T(4,128)} %param.13) | copy-start | bytes 1540
  168.6 97.2 %all-to-all-start.3 = ((bf16[8,8,32768]{2,1,0:T(8,128)(2,1)}), bf16[8,8,32768]{2,1,0:T(8,128)(2,1)}, u32[]{:S(2)}, u32[]{:S(2)}) async-start(bf16[8,8,32768]{2,1,0:T(8,128)(2,1)} %fusion.1), calls=%async_computation.3 | async-start | bytes 8388608 | tf_op jit(solution)/shard_map/all_to_all | solution.py:62
  173.3 162.9 %reduce-scatter.2.cloned.1.call-start = ((), (), s32[]{:S(2)}) async-start(), calls=%async_computation.6 | async-start | bytes 2621440 | tf_op jit(solution)/shard_map/reduce_scatter | solution.py:79
  265.9 3.6 copy-start
  306.4 106.1 %all-reduce.2.cloned.1.call-start = ((), (), s32[]{:S(2)}) async-start(), calls=%async_computation.7 | async-start | bytes 1048576 | tf_op jit(solution)/shard_map/psum | solution.py:87
Sparse Core Ops, SparseCore 0:
  9.5 24.1 all-gather.1
  306.5 29.6 reduce-scatter.1
  339.6 72.7 all-reduce.1
where the time goes:
time: 422 us; the launch traced here: 421 us
  waiting for transfers between devices  305 us (72%)
  matrix products  42.3 us (10%)
  local copies, waits for them, and re-layouts  32.4 us (8%)
  starting transfers between devices  22.1 us (5%)
  between operations  13.9 us (3%)
  other arithmetic  5.48 us (1%)
    all_to_all x1, waiting for transfers between devices, local(): lax.all_to_all(sending_back, 'dom', split_axis=0, concat_axis=0, tiled=True)  92.1 us
    all_to_all x1, waiting for transfers between devices, local(): lax.all_to_all(outgoing, 'dom', split_axis=0, concat_axis=0, tiled=True)  90.7 us
    psum x1, waiting for transfers between devices, local(): weight_grad = lax.psum(partial_grad, 'dom')  76.2 us
    reduce_scatter x1, waiting for transfers between devices, local(): lax.psum_scatter(lax.dot_general(own_rows, grad_proj, (((0,), (0,)), ((),...  29.7 us
    reshape x1, local copies, waits for them, and re-layouts, local(): products.reshape(slot_count * per_slot, tile_size, out_width)  17.6 us
    all_to_all x1, waiting for transfers between devices, local(): lax.all_to_all(feats, 'feat', split_axis=0, concat_axis=1, tiled=True)  15.2 us
    dot_general x1, matrix products, local(): jnp.einsum('bn,njh->bjh', source_hot, flat_products, precision=lax.Precis...  9.02 us
  transfers between devices with their start and end apart: 7, of which 5 were waited for; matrix products, arithmetic and copies ran while one was open for 7% of the time, Pallas kernels for 0%

commit v1 on v0

--- a/solution.py
+++ b/solution.py
@@ -2,6 +2,15 @@
 import jax.numpy as jnp
 from jax import lax
 from jax.sharding import PartitionSpec as P
+
+
+def doubling_sum(block, axis):
+    size = lax.axis_size(axis)
+    total, reach = (block, 1)
+    while reach < size:
+        total = total + lax.ppermute(total, axis, [(i, i ^ reach) for i in range(size)])
+        reach = 2 * reach
+    return total
 
 
 def local(feats, projection, tiles, slot_owner, slot_block, source_block, counts, out_grad):
@@ -84,7 +93,7 @@
         scatter_dimension=0,
         tiled=True,
     )
-    weight_grad = lax.psum(partial_grad, "dom")
+    weight_grad = doubling_sum(partial_grad, "dom")
     return (activated, weight_grad)
 
 

time: 422 us -> 397 us (0.941)
  waiting for transfers between devices: 305 us -> 274 us
  starting transfers between devices: 22.1 us -> 27.6 us
    psum x1 -> x0, waiting for transfers between devices: 76.2 us -> none  [local(): weight_grad = lax.psum(partial_grad, 'dom')]
    ppermute x0 -> x3, waiting for transfers between devices: none -> 44.9 us  [doubling_sum(): lax.ppermute(total, axis, [(i, i ^ reach) for i in range(size)])]
    ppermute x0 -> x3, starting transfers between devices: none -> 5.48 us  [doubling_sum(): lax.ppermute(total, axis, [(i, i ^ reach) for i in range(size)])]
  transfers between devices with their start and end apart: 7 -> 9, of which waited for: 5 -> 7; matrix products, arithmetic and copies ran while one was open for 7% -> 8% of each run, Pallas kernels for 0% -> 0%
where the time goes in v1:
time: 397 us; the launch traced here: 396 us
  waiting for transfers between devices  274 us (69%)
  matrix products  42.3 us (11%)
  local copies, waits for them, and re-layouts  31.4 us (8%)
  starting transfers between devices  27.6 us (7%)
  between operations  14.2 us (4%)
  other arithmetic  6.73 us (2%)
    all_to_all x1, waiting for transfers between devices, local(): lax.all_to_all(sending_back, 'dom', split_axis=0, concat_axis=0, tiled=True)  92.1 us
    all_to_all x1, waiting for transfers between devices, local(): lax.all_to_all(outgoing, 'dom', split_axis=0, concat_axis=0, tiled=True)  90.7 us
    ppermute x3, waiting for transfers between devices, doubling_sum(): lax.ppermute(total, axis, [(i, i ^ reach) for i in range(size)])  44.9 us
    reduce_scatter x1, waiting for transfers between devices, local(): lax.psum_scatter(lax.dot_general(own_rows, grad_proj, (((0,), (0,)), ((),...  29.8 us
    reshape x1, local copies, waits for them, and re-layouts, local(): products.reshape(slot_count * per_slot, tile_size, out_width)  17.7 us
    all_to_all x1, waiting for transfers between devices, local(): lax.all_to_all(feats, 'feat', split_axis=0, concat_axis=1, tiled=True)  15.2 us
    dot_general x1, matrix products, local(): jnp.einsum('bn,njh->bjh', source_hot, flat_products, precision=lax.Precis...  9.02 us
    dot_general x1, matrix products, local(): jnp.einsum('skij,sih->skjh', tiles, slot_grad, preferred_element_type=jnp...  8.11 us
  transfers between devices with their start and end apart: 9, of which 7 were waited for; matrix products, arithmetic and copies ran while one was open for 8% of the time, Pallas kernels for 0%

profile of v1, /device:TPU:0, one launch (start us, length us, event | category | flops | bytes accessed | tf_op | source)
XLA Modules:
  0.0 395.8 jit_solution(4329856704647381211)
XLA Ops:
  7.9 4.2 %all-to-all-start.1 = ((bf16[4,512,256]{2,1,0:T(8,128)(2,1)}), bf16[4,512,256]{2,1,0:T(8,128)(2,1)S(1)}, u32[]{:S(2)}, u32[]{:S(2)}) async-start(bf16[4,512,256]{2,1,0:T(8,128)(2,1)} %bitcast.67), calls=%async_computation.1 | async-start | bytes 2097152 | tf_op jit(solution)/shard_map/all_to_all | solution.py:26
  16.8 15.2 %all-to-all-done.1 = bf16[4,512,256]{2,1,0:T(8,128)(2,1)S(1)} async-done(((bf16[4,512,256]{2,1,0:T(8,128)(2,1)}), bf16[4,512,256]{2,1,0:T(8,128)(2,1)S(1)}, u32[]{:S(2)}, u32[]{:S(2)}) %all-to-all-start.1) | async-done | bytes 1048608 | tf_op jit(solution)/shard_map/all_to_all | solution.py:26
  32.0 6.8 %all-to-all-start = ((s32[8,1,8]{2,1,0:T(1,128)}), s32[8,1,8]{2,1,0:T(1,128)S(1)}, u32[]{:S(2)}, u32[]{:S(2)}) async-start(s32[8,1,8]{2,1,0:T(1,128)} %bitcast.2), calls=%async_computation | async-start | bytes 8192 | tf_op jit(solution)/shard_map/all_to_all | solution.py:53
  39.3 2.0 convolution_convert_fusion.3
  41.3 6.5 %gather_fusion = bf16[128,128,256]{2,1,0:T(8,128)(2,1)} fusion(bf16[4,128,256]{2,1,0:T(8,128)(2,1)S(1)} %bitcast.56, s32[1024]{0:T(1024)S(1)} %pad_clamp_fusion), kind=kCustom, calls=%fused_computation | custom fusion | bytes 16777728 | tf_op jit(solution)/shard_map/gather | solution.py:33
  47.8 7.0 %fusion.7 = bf16[32,128,256]{1,2,0:T(8,128)(2,1)S(1)} fusion(bf16[32,4,128,256]{3,2,1,0:T(8,128)(2,1)} %bitcast.58, bf16[32,4,128,128]{3,2,1,0:T(8,128)(2,1)} %param.10), kind=kOutput, calls=%fused_computation.13 | convolution fusion | flops 1074790400 | bytes 14680064 | tf_op jit(solution)/shard_map/skij,skjh->sih/dot_general | solution.py:34
  54.8 2.9 copy.58
  57.7 4.9 %fusion = bf16[8,8,32768]{2,1,0:T(8,128)(2,1)} fusion(bf16[32,32768]{1,0:T(8,128)(2,1)} %bitcast.61, s32[32]{0:T(128)S(1)} %multiply_add_fusion), kind=kOutput, calls=%fused_computation.3 | convolution fusion | flops 136316928 | bytes 6291584 | tf_op jit(solution)/shard_map/dot_general | solution.py:45
  62.6 6.2 %all-to-all-start.2 = ((bf16[8,8,32768]{2,1,0:T(8,128)(2,1)}), bf16[8,8,32768]{2,1,0:T(8,128)(2,1)}, u32[]{:S(2)}, u32[]{:S(2)}) async-start(bf16[8,8,32768]{2,1,0:T(8,128)(2,1)} %fusion), calls=%async_computation.2 | async-start | bytes 8388608 | tf_op jit(solution)/shard_map/all_to_all | solution.py:52
  70.1 90.7 %all-to-all-done.2 = bf16[8,8,32768]{2,1,0:T(8,128)(2,1)} async-done(((bf16[8,8,32768]{2,1,0:T(8,128)(2,1)}), bf16[8,8,32768]{2,1,0:T(8,128)(2,1)}, u32[]{:S(2)}, u32[]{:S(2)}) %all-to-all-start.2) | async-done | bytes 4194336 | tf_op jit(solution)/shard_map/all_to_all | solution.py:52
  160.8 2.8 fusion.3
  165.3 3.3 fusion.1
  168.6 4.7 %all-to-all-start.3 = ((bf16[8,8,32768]{2,1,0:T(8,128)(2,1)}), bf16[8,8,32768]{2,1,0:T(8,128)(2,1)}, u32[]{:S(2)}, u32[]{:S(2)}) async-start(bf16[8,8,32768]{2,1,0:T(8,128)(2,1)} %fusion.1), calls=%async_computation.3 | async-start | bytes 8388608 | tf_op jit(solution)/shard_map/all_to_all | solution.py:71
  173.7 92.1 %all-to-all-done.3 = bf16[8,8,32768]{2,1,0:T(8,128)(2,1)} async-done(((bf16[8,8,32768]{2,1,0:T(8,128)(2,1)}), bf16[8,8,32768]{2,1,0:T(8,128)(2,1)}, u32[]{:S(2)}, u32[]{:S(2)}) %all-to-all-start.3) | async-done | bytes 4194336 | tf_op jit(solution)/shard_map/all_to_all | solution.py:71
  265.9 3.1 convolution_convert_fusion.2
  269.5 8.1 %fusion.5 = f32[32,256,4,128]{3,1,2,0:T(8,128)} fusion(bf16[32,4,128,128]{3,2,1,0:T(8,128)(2,1)S(1)} %copy-done, bf16[32,128,256]{2,1,0:T(8,128)(2,1)S(1)} %bitcast.62), kind=kOutput, calls=%fused_computation.10 | convolution fusion | flops 1073741824 | bytes 23068672 | tf_op jit(solution)/shard_map/skij,sih->skjh/dot_general | solution.py:78
  277.6 17.7 %copy.51 = f32[128,128,256]{2,0,1:T(8,128)} copy(f32[128,128,256]{1,2,0:T(8,128)} %bitcast.57) | data formatting | bytes 33554432 | tf_op jit(solution)/shard_map/reshape | solution.py:82
  295.3 9.0 %convolution_convert_fusion.4 = bf16[4,128,256]{2,0,1:T(4,128)(2,1)S(1)} fusion(f32[128,128,256]{2,0,1:T(8,128)} %copy.51, s32[128]{0:T(128)S(1)} %eq.67), kind=kOutput, calls=%fused_computation.15 | convolution fusion | flops 201458176 | bytes 17039872 | tf_op jit(solution)/shard_map/bn,njh->bjh/dot_general | solution.py:83
  304.4 2.1 convolution_bitcast_fusion
  306.5 29.8 %reduce-scatter.2.cloned.1.call-done = f32[256,512]{0,1:T(8,128)} async-done(((f32[1024,512]{0,1:T(8,128)}), f32[256,512]{0,1:T(8,128)}) %reduce-scatter.2.cloned.1.call-update) | async-done | bytes 524304 | tf_op jit(solution)/shard_map/reduce_scatter | solution.py:88
  337.8 12.2 %collective-permute-done = f32[256,512]{0,1:T(8,128)S(1)} collective-permute-done((f32[256,512]{0,1:T(8,128)}, f32[256,512]{0,1:T(8,128)S(1)}, u32[]{:S(2)}, u32[]{:S(2)}) %collective-permute-start) | collective-permute-done | bytes 524320 | tf_op jit(solution)/shard_map/ppermute | solution.py:11
  352.6 11.2 %collective-permute-done.1 = f32[256,512]{0,1:T(8,128)S(1)} collective-permute-done((f32[256,512]{0,1:T(8,128)S(1)}, f32[256,512]{0,1:T(8,128)S(1)}, u32[]{:S(2)}, u32[]{:S(2)}) %collective-permute-start.1) | collective-permute-done | bytes 524320 | tf_op jit(solution)/shard_map/ppermute | solution.py:11
  363.9 2.5 collective-permute-start.2
  366.4 21.5 %collective-permute-done.2 = f32[256,512]{0,1:T(8,128)S(1)} collective-permute-done((f32[256,512]{0,1:T(8,128)S(1)}, f32[256,512]{0,1:T(8,128)S(1)}, u32[]{:S(2)}, u32[]{:S(2)}) %collective-permute-start.2) | collective-permute-done | bytes 524320 | tf_op jit(solution)/shard_map/ppermute | solution.py:11
  (49 shorter events, 15.0 us)
Async XLA Ops:
  7.2 32.2 %all-gather.2.cloned.1.call-start = ((), (), s32[]{:S(2)}) async-start(), calls=%async_computation.5 | async-start | bytes 1310720 | tf_op jit(solution)/shard_map/all_gather | solution.py:27
  7.9 24.1 %all-to-all-start.1 = ((bf16[4,512,256]{2,1,0:T(8,128)(2,1)}), bf16[4,512,256]{2,1,0:T(8,128)(2,1)S(1)}, u32[]{:S(2)}, u32[]{:S(2)}) async-start(bf16[4,512,256]{2,1,0:T(8,128)(2,1)} %bitcast.67), calls=%async_computation.1 | async-start | bytes 2097152 | tf_op jit(solution)/shard_map/all_to_all | solution.py:26
  32.0 30.6 %all-to-all-start = ((s32[8,1,8]{2,1,0:T(1,128)}), s32[8,1,8]{2,1,0:T(1,128)S(1)}, u32[]{:S(2)}, u32[]{:S(2)}) async-start(s32[8,1,8]{2,1,0:T(1,128)} %bitcast.2), calls=%async_computation | async-start | bytes 8192 | tf_op jit(solution)/shard_map/all_to_all | solution.py:53
  41.3 6.5 %copy-start.1 = (bf16[512,512]{1,0:T(8,128)(2,1)}, bf16[512,512]{1,0:T(8,128)(2,1)S(1)}, u32[]{:S(2)}) copy-start(bf16[512,512]{1,0:T(8,128)(2,1)S(1)} %convolution_convert_fusion.3) | copy-start | bytes 1572868
  62.6 6.2 %copy-start.5 = (s32[512]{0:T(512)S(1)}, s32[512]{0:T(512)}, u32[]{:S(2)}) copy-start(s32[512]{0:T(512)} %param.14) | copy-start | bytes 6148
  62.6 98.2 %all-to-all-start.2 = ((bf16[8,8,32768]{2,1,0:T(8,128)(2,1)}), bf16[8,8,32768]{2,1,0:T(8,128)(2,1)}, u32[]{:S(2)}, u32[]{:S(2)}) async-start(bf16[8,8,32768]{2,1,0:T(8,128)(2,1)} %fusion), calls=%async_computation.2 | async-start | bytes 8388608 | tf_op jit(solution)/shard_map/all_to_all | solution.py:52
  68.8 95.2 %copy-start.2 = (bf16[512,512]{1,0:T(8,128)(2,1)S(1)}, bf16[512,512]{1,0:T(8,128)(2,1)}, u32[]{:S(2)}) copy-start(bf16[512,512]{1,0:T(8,128)(2,1)} %copy-done.1) | copy-start | bytes 1572868
  68.8 95.2 %copy-start.3 = (bf16[512,256]{1,0:T(8,128)(2,1)S(1)}, bf16[512,256]{1,0:T(8,128)(2,1)}, u32[]{:S(2)}) copy-start(bf16[512,256]{1,0:T(8,128)(2,1)} %param.15) | copy-start | bytes 786436
  168.6 4.9 %copy-start.4 = (s32[32,4]{0,1:T(4,128)S(1)}, s32[32,4]{0,1:T(4,128)}, u32[]{:S(2)}) copy-start(s32[32,4]{0,1:T(4,128)} %param.13) | copy-start | bytes 1540
  168.6 97.2 %all-to-all-start.3 = ((bf16[8,8,32768]{2,1,0:T(8,128)(2,1)}), bf16[8,8,32768]{2,1,0:T(8,128)(2,1)}, u32[]{:S(2)}, u32[]{:S(2)}) async-start(bf16[8,8,32768]{2,1,0:T(8,128)(2,1)} %fusion.1), calls=%async_computation.3 | async-start | bytes 8388608 | tf_op jit(solution)/shard_map/all_to_all | solution.py:71
  173.3 163.0 %reduce-scatter.2.cloned.1.call-start = ((), (), s32[]{:S(2)}) async-start(), calls=%async_computation.6 | async-start | bytes 2621440 | tf_op jit(solution)/shard_map/reduce_scatter | solution.py:88
  265.9 3.6 copy-start
  336.3 13.7 %collective-permute-start = (f32[256,512]{0,1:T(8,128)}, f32[256,512]{0,1:T(8,128)S(1)}, u32[]{:S(2)}, u32[]{:S(2)}) collective-permute-start(f32[256,512]{0,1:T(8,128)} %reduce-scatter.2.cloned.1.call-done), channel_id=1, source_target_pairs={{0,4},{4,0},{8,12},{12,8},{16,20},{20,16},{24,28},{28,24},{1,5},{5... | collective-permute-start | bytes 1572872 | tf_op jit(solution)/shard_map/ppermute | solution.py:11
  351.1 12.7 %collective-permute-start.1 = (f32[256,512]{0,1:T(8,128)S(1)}, f32[256,512]{0,1:T(8,128)S(1)}, u32[]{:S(2)}, u32[]{:S(2)}) collective-permute-start(f32[256,512]{0,1:T(8,128)S(1)} %add.65), channel_id=1, source_target_pairs={{0,8},{4,12},{8,0},{12,4},{16,24},{20,28},{24,16},{28,20},{1,9},{5... | collective-permute-start | bytes 1572872 | tf_op jit(solution)/shard_map/ppermute | solution.py:11
  363.9 24.0 %collective-permute-start.2 = (f32[256,512]{0,1:T(8,128)S(1)}, f32[256,512]{0,1:T(8,128)S(1)}, u32[]{:S(2)}, u32[]{:S(2)}) collective-permute-start(f32[256,512]{0,1:T(8,128)S(1)} %add.66), channel_id=1, source_target_pairs={{0,16},{4,20},{8,24},{12,28},{16,0},{20,4},{24,8},{28,12},{1,17},{... | collective-permute-start | bytes 1572872 | tf_op jit(solution)/shard_map/ppermute | solution.py:11
Sparse Core Ops, SparseCore 0:
  9.5 24.1 all-gather.1
  306.6 29.6 reduce-scatter.1
